TPU v7x, 128 devices: a whole 4x4x4 slice. The times are simulated.
128 devices in a mesh: dp: 16 (over z, y), ctx: 8 (over x, core).
Axes of the slice: x: 4, y: 4, z: 4, core: 2. Of those that a mesh axis runs over, the one named last changes fastest.
Arguments:
- hidden_in: bfloat16 [16384, 960], P(('dp', 'ctx')), may hold values from -6 to 6
- out_grad: bfloat16 [16384, 960], P(('dp', 'ctx')), may hold values from -6 to 6
- norm_gains: bfloat16 [2, 960], P(None, 'dp'), may hold values from 0.5 to 1.5
- q_weight: bfloat16 [960, 960], P('dp'), may hold values from -0.1875 to 0.1875
- k_weight: bfloat16 [960, 320], P('dp'), may hold values from -0.1875 to 0.1875
- v_weight: bfloat16 [960, 320], P('dp'), may hold values from -0.1875 to 0.1875
- out_weight: bfloat16 [960, 960], P('dp'), may hold values from -0.75 to 0.75
- gate_weight: bfloat16 [960, 2560], P('dp'), may hold values from -0.1875 to 0.1875
- up_weight: bfloat16 [960, 2560], P('dp'), may hold values from -0.1875 to 0.1875
- down_weight: bfloat16 [960, 2560], P('dp'), may hold values from -0.125 to 0.125
Outputs:
- hidden_out: bfloat16 [16384, 960], P(('dp', 'ctx'))
- in_grad: float32 [16384, 960], P(('dp', 'ctx'))
- gains_grad: float32 [2, 960], P(None, 'dp')
- q_weight_grad: float32 [960, 960], P('dp')
- k_weight_grad: float32 [960, 320], P('dp')
- v_weight_grad: float32 [960, 320], P('dp')
- out_weight_grad: float32 [960, 960], P('dp')
- gate_weight_grad: float32 [960, 2560], P('dp')
- up_weight_grad: float32 [960, 2560], P('dp')
- down_weight_grad: float32 [960, 2560], P('dp')
All inputs are finite; a program needn't handle non-finite values.
Results may differ from a plain program's by a relative error of at most 0.015.
Values may be sent and summed in bfloat16 or wider, within the bound.
No kernel may reach another device: no remote copies, remote signals or barrier semaphores. Data moves between devices by JAX's collectives and lax.ppermute only.
A program may use at most 192 MiB of HBM per device.

v0:
```python
import math
import jax
import jax.numpy as jnp
from jax import lax
from jax.sharding import PartitionSpec as P

HEADS = 15
KV_HEADS = 5
HEAD_DIM = 64
EPS = 1e-05
ROPE_BASE = 100000.0
NEG_FILL = -1e30


def passed_along(block, axis, distance):
    devices = range(lax.axis_size(axis))
    route = [((i - distance) % len(devices), i) for i in devices]
    return lax.ppermute(block, axis, route)


def shifted(block, axis, distance):
    devices = range(lax.axis_size(axis))
    route = [(i - distance, i) for i in devices if i - distance in devices]
    return lax.ppermute(block, axis, route)


def rotary(positions, head_size):
    half = head_size // 2
    freq = ROPE_BASE ** (-(jnp.arange(half, dtype=jnp.float32) * 2.0) / head_size)
    angles = positions[:, None] * freq[None, :]
    return (
        jnp.concatenate([jnp.cos(angles), jnp.cos(angles)], axis=1),
        jnp.concatenate([jnp.sin(angles), jnp.sin(angles)], axis=1),
    )


def rotate(values, cosine, sine, sign):
    half = values.shape[-1] // 2
    turned = jnp.concatenate([-values[..., half:], values[..., :half]], axis=-1)
    return values * cosine[:, None, :] + sign * turned * sine[:, None, :]


def norm_forward(values):
    scale = lax.rsqrt(jnp.mean(values * values, axis=1, keepdims=True) + EPS)
    return (values * scale, scale)


def norm_backward(grad_normed, normed, scale, gain):
    weighted = grad_normed * gain
    inner = jnp.mean(weighted * normed, axis=1, keepdims=True)
    return (scale * (weighted - normed * inner), jnp.sum(grad_normed * normed, axis=0))


def contract_rows(left, right):
    return lax.dot_general(
        left, right, (((0,), (0,)), ((), ())), preferred_element_type=jnp.float32
    )


def contract_cols(left, right):
    return lax.dot_general(
        left, right, (((1,), (1,)), ((), ())), preferred_element_type=jnp.float32
    )


def on_device(
    hidden_in,
    out_grad,
    norm_gains,
    q_weight,
    k_weight,
    v_weight,
    out_weight,
    gate_weight,
    up_weight,
    down_weight,
):
    rows = hidden_in.shape[0]
    ctx_count = lax.axis_size("ctx")
    ctx_index = lax.axis_index("ctx")
    groups = HEADS // KV_HEADS
    kv_width = KV_HEADS * HEAD_DIM
    scaling = 1.0 / math.sqrt(HEAD_DIM)
    shards = (
        norm_gains,
        q_weight,
        k_weight,
        v_weight,
        out_weight,
        gate_weight,
        up_weight,
        down_weight,
    )
    gathered = (
        lax.all_gather(shards[0], "dp", axis=1, tiled=True),
        lax.all_gather(shards[1], "dp", axis=0, tiled=True),
        lax.all_gather(shards[2], "dp", axis=0, tiled=True),
        lax.all_gather(shards[3], "dp", axis=0, tiled=True),
        lax.all_gather(shards[4], "dp", axis=0, tiled=True),
        lax.all_gather(shards[5], "dp", axis=0, tiled=True),
        lax.all_gather(shards[6], "dp", axis=0, tiled=True),
        lax.all_gather(shards[7], "dp", axis=0, tiled=True),
    )
    gain_rows, query_mat, key_mat, value_mat, output_mat, gate_mat, up_mat, down_mat = gathered
    gain_first = gain_rows[0].astype(jnp.float32)
    gain_second = gain_rows[1].astype(jnp.float32)
    query_pos = ctx_index * rows + jnp.arange(rows, dtype=jnp.int32)
    cosine, sine = rotary(query_pos.astype(jnp.float32), HEAD_DIM)
    inputs_wide = hidden_in.astype(jnp.float32)
    normed_one, scale_one = norm_forward(inputs_wide)
    first_in = (normed_one * gain_first).astype(jnp.bfloat16)
    queries = jnp.dot(first_in, query_mat, preferred_element_type=jnp.float32).reshape(
        rows, HEADS, HEAD_DIM
    )
    queries = (
        rotate(queries, cosine, sine, 1.0)
        .astype(jnp.bfloat16)
        .reshape(rows, KV_HEADS, groups, HEAD_DIM)
    )
    keys = jnp.dot(first_in, key_mat, preferred_element_type=jnp.float32).reshape(
        rows, KV_HEADS, HEAD_DIM
    )
    keys = rotate(keys, cosine, sine, 1.0).astype(jnp.bfloat16).reshape(rows, kv_width)
    values = jnp.dot(first_in, value_mat, preferred_element_type=jnp.float32).astype(jnp.bfloat16)
    key_value = jnp.concatenate([keys, values], axis=1)
    piece = lax.all_gather(key_value, "ctx", axis=0, tiled=True)
    peak = jnp.full((KV_HEADS, groups, rows), NEG_FILL, jnp.float32)
    count = piece.shape[0]
    attend_block_keys = piece[:, :kv_width].reshape(count, KV_HEADS, HEAD_DIM)
    attend_block_values = piece[:, kv_width:].reshape(count, KV_HEADS, HEAD_DIM)
    attend_key_pos = jnp.arange(count, dtype=jnp.int32)
    attend_allowed = attend_key_pos[None, :] <= query_pos[:, None]
    attend_scores = (
        jnp.einsum("skgd,pkd->kgsp", queries, attend_block_keys, preferred_element_type=jnp.float32)
        * scaling
    )
    attend_scores = jnp.where(attend_allowed, attend_scores, NEG_FILL)
    new_peak = jnp.maximum(peak, jnp.max(attend_scores, axis=3))
    weights = jnp.where(attend_allowed, jnp.exp(attend_scores - new_peak[..., None]), 0.0)
    total = jnp.sum(weights, axis=3)
    added = jnp.einsum(
        "kgsp,pkd->skgd",
        weights.astype(jnp.bfloat16),
        attend_block_values,
        preferred_element_type=jnp.float32,
    )
    accum = added
    peak, total, accum = (new_peak, total, accum)
    lse = peak + jnp.log(total)
    attn = (
        (accum / jnp.transpose(total, (2, 0, 1))[..., None])
        .astype(jnp.bfloat16)
        .reshape(rows, HEADS * HEAD_DIM)
    )
    middle = inputs_wide + contract_cols(attn, output_mat)
    normed_two, scale_two = norm_forward(middle)
    second_in = (normed_two * gain_second).astype(jnp.bfloat16)
    gate = jnp.dot(second_in, gate_mat, preferred_element_type=jnp.float32)
    up_part = jnp.dot(second_in, up_mat, preferred_element_type=jnp.float32)
    sigma = jax.nn.sigmoid(gate)
    hidden = (gate * sigma * up_part).astype(jnp.bfloat16)
    hidden_out = (middle + contract_cols(hidden, down_mat)).astype(jnp.bfloat16)
    regathered = (
        lax.all_gather(shards[0], "dp", axis=1, tiled=True),
        lax.all_gather(shards[1], "dp", axis=0, tiled=True),
        lax.all_gather(shards[2], "dp", axis=0, tiled=True),
        lax.all_gather(shards[3], "dp", axis=0, tiled=True),
        lax.all_gather(shards[4], "dp", axis=0, tiled=True),
        lax.all_gather(shards[5], "dp", axis=0, tiled=True),
        lax.all_gather(shards[6], "dp", axis=0, tiled=True),
        lax.all_gather(shards[7], "dp", axis=0, tiled=True),
    )
    gain_rows, query_mat, key_mat, value_mat, output_mat, gate_mat, up_mat, down_mat = regathered
    gain_first = gain_rows[0].astype(jnp.float32)
    gain_second = gain_rows[1].astype(jnp.float32)
    grad_hidden = jnp.dot(out_grad, down_mat, preferred_element_type=jnp.float32)
    grad_gate = (grad_hidden * up_part * sigma * (1.0 + gate * (1.0 - sigma))).astype(jnp.bfloat16)
    grad_up = (grad_hidden * gate * sigma).astype(jnp.bfloat16)
    down_term = contract_rows(out_grad, hidden)
    gate_term = contract_rows(second_in, grad_gate)
    up_term = contract_rows(second_in, grad_up)
    grad_second = contract_cols(grad_gate, gate_mat) + contract_cols(grad_up, up_mat)
    back_two, gain_two_term = norm_backward(grad_second, normed_two, scale_two, gain_second)
    grad_middle = out_grad.astype(jnp.float32) + back_two
    middle_low = grad_middle.astype(jnp.bfloat16)
    output_term = contract_rows(middle_low, attn)
    grad_attn = jnp.dot(middle_low, output_mat, preferred_element_type=jnp.float32).astype(
        jnp.bfloat16
    )
    grad_heads = grad_attn.reshape(rows, KV_HEADS, groups, HEAD_DIM)
    attn_heads = attn.reshape(rows, KV_HEADS, groups, HEAD_DIM)
    delta = jnp.transpose(
        jnp.sum(grad_heads.astype(jnp.float32) * attn_heads.astype(jnp.float32), axis=3), (1, 2, 0)
    )
    travel = key_value
    carried = jnp.zeros((rows, 2 * kv_width), jnp.float32)
    grad_queries = jnp.zeros((rows, KV_HEADS, groups, HEAD_DIM), jnp.float32)
    for step in range(ctx_count):
        owner = (ctx_index - step) % ctx_count
        key_pos = owner * rows + jnp.arange(rows, dtype=jnp.int32)
        allowed = key_pos[None, :] <= query_pos[:, None]
        block_keys = travel[:, :kv_width].reshape(rows, KV_HEADS, HEAD_DIM)
        block_values = travel[:, kv_width:].reshape(rows, KV_HEADS, HEAD_DIM)
        scores = (
            jnp.einsum("skgd,pkd->kgsp", queries, block_keys, preferred_element_type=jnp.float32)
            * scaling
        )
        probs = jnp.exp(jnp.where(allowed, scores - lse[..., None], NEG_FILL))
        value_grad = jnp.einsum(
            "kgsp,skgd->pkd",
            probs.astype(jnp.bfloat16),
            grad_heads,
            preferred_element_type=jnp.float32,
        )
        prob_grad = jnp.einsum(
            "skgd,pkd->kgsp", grad_heads, block_values, preferred_element_type=jnp.float32
        )
        score_grad = (probs * (prob_grad - delta[..., None]) * scaling).astype(jnp.bfloat16)
        grad_queries = grad_queries + jnp.einsum(
            "kgsp,pkd->skgd", score_grad, block_keys, preferred_element_type=jnp.float32
        )
        key_grad = jnp.einsum(
            "kgsp,skgd->pkd", score_grad, queries, preferred_element_type=jnp.float32
        )
        carried = carried + jnp.concatenate(
            [key_grad.reshape(rows, kv_width), value_grad.reshape(rows, kv_width)], axis=1
        )
        carried = passed_along(carried, "ctx", 1)
        if step + 1 < ctx_count:
            travel = shifted(travel, "ctx", 1)
    key_low = rotate(carried[:, :kv_width].reshape(rows, KV_HEADS, HEAD_DIM), cosine, sine, -1.0)
    key_low = key_low.astype(jnp.bfloat16).reshape(rows, kv_width)
    value_low = carried[:, kv_width:].astype(jnp.bfloat16)
    query_low = rotate(grad_queries.reshape(rows, HEADS, HEAD_DIM), cosine, sine, -1.0)
    query_low = query_low.astype(jnp.bfloat16).reshape(rows, HEADS * HEAD_DIM)
    query_term = contract_rows(first_in, query_low)
    key_term = contract_rows(first_in, key_low)
    value_term = contract_rows(first_in, value_low)
    grad_first = (
        contract_cols(query_low, query_mat)
        + contract_cols(key_low, key_mat)
        + contract_cols(value_low, value_mat)
    )
    back_one, gain_one_term = norm_backward(grad_first, normed_one, scale_one, gain_first)
    in_grad = grad_middle + back_one
    terms = (query_term, key_term, value_term, output_term, gate_term, up_term, down_term)
    stacked = jnp.concatenate(terms, axis=1)
    gain_terms = jnp.stack([gain_one_term, gain_two_term])
    own_grads, own_gains = (
        lax.psum_scatter(stacked, "dp", scatter_dimension=0, tiled=True),
        lax.psum_scatter(gain_terms, "dp", scatter_dimension=1, tiled=True),
    )
    own_grads, own_gains = lax.psum((own_grads, own_gains), "ctx")
    results = []
    offset = 0
    for term in terms:
        width = term.shape[1]
        results.append(own_grads[:, offset : offset + width])
        offset = offset + width
    return (
        hidden_out,
        in_grad,
        own_gains,
        results[0],
        results[1],
        results[2],
        results[3],
        results[4],
        results[5],
        results[6],
    )


def solution(mesh):
    return jax.shard_map(
        on_device,
        mesh=mesh,
        in_specs=(
            P(("dp", "ctx"), None),
            P(("dp", "ctx"), None),
            P(None, "dp"),
            P("dp", None),
            P("dp", None),
            P("dp", None),
            P("dp", None),
            P("dp", None),
            P("dp", None),
            P("dp", None),
        ),
        out_specs=(
            P(("dp", "ctx"), None),
            P(("dp", "ctx"), None),
            P(None, "dp"),
            P("dp", None),
            P("dp", None),
            P("dp", None),
            P("dp", None),
            P("dp", None),
            P("dp", None),
            P("dp", None),
        ),
        check_vma=False,
    )
```

profile of v0, /device:TPU:0, one launch (start us, length us, event | category | flops | bytes accessed | tf_op | source)
XLA Modules:
  0.0 1019.9 jit_solution(10856639301617734905)
XLA Ops:
  7.3 26.2 %all-gather.2 = bf16[16,60,320]{2,1,0:T(8,128)(2,1)S(1)} all-gather(bf16[1,60,320]{2,1,0:T(8,128)(2,1)} %bitcast.615), channel_id=1, replica_groups=mesh['dp'=16,'ctx'=8] {'dp'}, dimensions={0}, use_global_device_ids=true | all-gather | bytes 652800 | tf_op jit(solution)/shard_map/all_gather | solution.py:98
  33.7 19.7 %all-gather = bf16[16,60,2]{1,2,0:T(2,128)(2,1)S(1)} all-gather(bf16[1,60,2]{1,2,0:T(2,128)(2,1)} %bitcast.621), channel_id=1, replica_groups=mesh['dp'=16,'ctx'=8] {'dp'}, dimensions={0}, use_global_device_ids=true | all-gather | bytes 4080 | tf_op jit(solution)/shard_map/all_gather | solution.py:95
  55.2 22.4 %all-gather.1 = bf16[16,60,320]{2,1,0:T(8,128)(2,1)S(1)} all-gather(bf16[1,60,320]{2,1,0:T(8,128)(2,1)} %bitcast.616), channel_id=1, replica_groups=mesh['dp'=16,'ctx'=8] {'dp'}, dimensions={0}, use_global_device_ids=true | all-gather | bytes 652800 | tf_op jit(solution)/shard_map/all_gather | solution.py:97
  86.6 5.5 collective-permute-start.1
  93.1 5.5 collective-permute-start.2
  99.6 6.1 collective-permute-start.3
  106.7 5.6 collective-permute-start.4
  113.3 5.6 collective-permute-start.5
  120.0 6.1 collective-permute-start.6
  127.4 2.2 fusion.138
  129.6 24.0 %all-gather.19.cloned.1.call-done = bf16[16,60,960]{2,1,0:T(8,128)(2,1)} async-done(((bf16[1,60,960]{2,1,0:T(8,128)(2,1)}), bf16[16,60,960]{2,1,0:T(8,128)(2,1)}) %all-gather.19.cloned.1.call-update) | async-done | bytes 1843216 | tf_op jit(solution)/shard_map/all_gather | solution.py:99
  153.7 4.0 reshape.296
  157.6 42.5 %all-gather.17.cloned.1.call-done = bf16[16,60,960]{2,1,0:T(8,128)(2,1)} async-done(((bf16[1,60,960]{2,1,0:T(8,128)(2,1)}), bf16[16,60,960]{2,1,0:T(8,128)(2,1)}) %all-gather.17.cloned.1.call-update) | async-done | bytes 1843216 | tf_op jit(solution)/shard_map/all_gather | solution.py:96
  200.1 2.8 reshape.294
  208.1 2.1 fusion.78
  222.1 35.6 %all-gather.21.cloned.1.call-done = bf16[16,60,2560]{2,1,0:T(8,128)(2,1)} async-done(((bf16[1,60,2560]{2,1,0:T(8,128)(2,1)}), bf16[16,60,2560]{2,1,0:T(8,128)(2,1)}) %all-gather.21.cloned.1.call-update) | async-done | bytes 4915216 | tf_op jit(solution)/shard_map/all_gather | solution.py:100
  257.7 7.3 reshape.298
  265.1 50.6 %all-gather.23.cloned.1.call-done = bf16[16,60,2560]{2,1,0:T(8,128)(2,1)} async-done(((bf16[1,60,2560]{2,1,0:T(8,128)(2,1)}), bf16[16,60,2560]{2,1,0:T(8,128)(2,1)}) %all-gather.23.cloned.1.call-update) | async-done | bytes 4915216 | tf_op jit(solution)/shard_map/all_gather | solution.py:101
  315.7 7.3 reshape.300
  323.0 4.5 fusion.147
  329.5 44.1 %all-gather.25.cloned.1.call-done = bf16[16,60,2560]{2,1,0:T(8,128)(2,1)} async-done(((bf16[1,60,2560]{2,1,0:T(8,128)(2,1)}), bf16[16,60,2560]{2,1,0:T(8,128)(2,1)}) %all-gather.25.cloned.1.call-update) | async-done | bytes 4915216 | tf_op jit(solution)/shard_map/all_gather | solution.py:102
  373.6 7.5 reshape.302
  381.2 4.7 multiply_convert_fusion
  387.4 4.1 multiply_reduce_fusion
  394.1 5.1 fusion.159
  399.1 5.2 fusion.160
  409.8 5.3 convolution_bitcast_fusion
  418.6 6.7 collective-permute-done.8
  426.0 7.0 collective-permute-done.9
  433.6 7.1 collective-permute-done.10
  441.2 7.3 collective-permute-done.11
  449.1 7.2 collective-permute-done.12
  456.4 2.5 fusion.116
  458.9 5.1 collective-permute-done.13
  464.1 2.7 fusion.128
  466.8 5.0 collective-permute-done.14
  473.9 41.3 %concatenate.70 = f32[960,10240]{1,0:T(8,128)} concatenate(f32[960,960]{1,0:T(8,128)} %fusion.128, f32[960,320]{1,0:T(8,128)S(1)} %fusion.126, f32[960,320]{1,0:T(8,128)} %fusion.120, f32[960,960]{1,0:T(8,128)} %fusion.116, f32[960,2560]{1,0:T(8,128)} %fusion.159, f32[960,2560]{1,0:T(8,128)} %fusion.160, f32[960,2560]{1,0:T(8,128)} %convolution_bitcast_fusion), dimensions={1} | concatenate | bytes 78643200 | tf_op jit(solution)/shard_map/concatenate | solution.py:247
  515.2 344.0 %fusion = f32[64,10240]{1,0:T(8,128)S(1)} fusion(f32[960,10240]{1,0:T(8,128)} %concatenate.70), kind=kCustom, calls=%all-reduce-scatter | all-reduce-scatter fusion | flops 10485761 | bytes 41943552
  860.9 3.5 collective-permute-start.15
  866.3 3.0 fusion.161
  869.3 4.7 fusion.74
  874.1 43.8 %collective-permute-done.15 = f32[60,10240]{1,0:T(8,128)} collective-permute-done((f32[60,10240]{1,0:T(8,128)}, f32[60,10240]{1,0:T(8,128)}, u32[]{:S(2)}, u32[]{:S(2)}) %collective-permute-start.15) | collective-permute-done | bytes 2457632
  917.9 15.5 %concatenate.71 = f32[124,10240]{1,0:T(8,128)} concatenate(f32[60,10240]{1,0:T(8,128)} %collective-permute-done.15, f32[64,10240]{1,0:T(8,128)S(1)} %fusion), dimensions={0} | concatenate | bytes 10158080
  933.4 3.7 constant_dynamic-slice_fusion
  938.1 40.0 %all-reduce = f32[2,960]{1,0:T(2,128)S(1)} all-reduce(f32[2,960]{1,0:T(2,128)S(1)} %pad_maximum_fusion.4), channel_id=2, replica_groups=mesh['dp'=16,'ctx'=8] {'dp'}, use_global_device_ids=true, to_apply=%region_9.10.clone | all-reduce | flops 1920 | bytes 15360
  978.2 13.0 %psum.14 = f32[2,60]{1,0:T(2,128)} all-reduce(f32[2,60]{1,0:T(2,128)S(1)} %constant_dynamic-slice_fusion.1), channel_id=1, replica_groups=mesh['dp'=16,'ctx'=8] {'ctx'}, use_global_device_ids=true, to_apply=%region_10.11 | all-reduce | flops 120 | bytes 960 | tf_op jit(solution)/shard_map/psum | solution.py:253
  992.1 14.3 %all-reduce.5.cloned.1.call-done = f32[60,10240]{1,0:T(8,128)} async-done(((f32[60,10240]{1,0:T(8,128)}), f32[60,10240]{1,0:T(8,128)}) %all-reduce.5.cloned.1.call-update) | async-done | bytes 2457616 | tf_op jit(solution)/shard_map/psum | solution.py:253
  1010.1 2.8 fusion.135
  (286 shorter events, 60.8 us)
Async XLA Ops:
  7.2 70.8 %copy-start.1 = (bf16[128,960]{0,1:T(8,128)(2,1)S(1)}, bf16[128,960]{0,1:T(8,128)(2,1)}, u32[]{:S(2)}) copy-start(bf16[128,960]{0,1:T(8,128)(2,1)} %param.10) | copy-start | bytes 737284
  7.2 120.2 %all-gather.15.cloned.1.call-start = ((), (), s32[]{:S(2)}) async-start(), calls=%async_computation | async-start | bytes 1474560 | tf_op jit(solution)/shard_map/all_gather | solution.py:126
  33.7 79.3 %copy-start.17 = (bf16[960,320]{1,0:T(8,128)(2,1)}, bf16[960,320]{1,0:T(8,128)(2,1)S(1)}, u32[]{:S(2)}) copy-start(bf16[960,320]{1,0:T(8,128)(2,1)S(1)} %reshape.292) | copy-start | bytes 1843204
  54.1 25.9 %copy-start.53 = (f32[1,960]{1,0:T(1,128)}, f32[1,960]{1,0:T(1,128)S(1)}, u32[]{:S(2)}) copy-start(f32[1,960]{1,0:T(1,128)S(1)} %get-tuple-element.53) | copy-start | bytes 11524
  55.2 24.0 %copy-start.56 = (f32[128]{0:T(128)}, f32[128]{0:T(128)S(1)}, u32[]{:S(2)}) copy-start(f32[128]{0:T(128)S(1)} %add_rsqrt_fusion.1) | copy-start | bytes 1540
  77.9 51.7 %copy-start.7 = (bf16[960,320]{1,0:T(8,128)(2,1)}, bf16[960,320]{1,0:T(8,128)(2,1)S(1)}, u32[]{:S(2)}) copy-start(bf16[960,320]{1,0:T(8,128)(2,1)S(1)} %reshape.290) | copy-start | bytes 1843204
  78.6 51.1 %copy-start.29 = (bf16[128,320]{0,1:T(8,128)(2,1)}, bf16[128,320]{0,1:T(8,128)(2,1)S(1)}, u32[]{:S(2)}) copy-start(bf16[128,320]{0,1:T(8,128)(2,1)S(1)} %convolution_convert_fusion.1) | copy-start | bytes 245764
  81.4 72.3 %all-gather.19.cloned.1.call-start = ((), (), s32[]{:S(2)}) async-start(), calls=%async_computation.3 | async-start | bytes 2228224 | tf_op jit(solution)/shard_map/all_gather | solution.py:99
  82.1 118.0 %all-gather.17.cloned.1.call-start = ((), (), s32[]{:S(2)}) async-start(), calls=%async_computation.2 | async-start | bytes 2228224 | tf_op jit(solution)/shard_map/all_gather | solution.py:96
  82.9 174.9 %all-gather.21.cloned.1.call-start = ((), (), s32[]{:S(2)}) async-start(), calls=%async_computation.4 | async-start | bytes 5570560 | tf_op jit(solution)/shard_map/all_gather | solution.py:100
  83.5 232.2 %all-gather.23.cloned.1.call-start = ((), (), s32[]{:S(2)}) async-start(), calls=%async_computation.5 | async-start | bytes 5570560 | tf_op jit(solution)/shard_map/all_gather | solution.py:101
  84.0 289.6 %all-gather.25.cloned.1.call-start = ((), (), s32[]{:S(2)}) async-start(), calls=%async_computation.6 | async-start | bytes 5570560 | tf_op jit(solution)/shard_map/all_gather | solution.py:102
  84.1 2.5 collective-permute-start
  85.4 921.0 %all-reduce.5.cloned.1.call-start = ((), (), s32[]{:S(2)}) async-start(), calls=%async_computation.1 | async-start | bytes 5242880 | tf_op jit(solution)/shard_map/psum | solution.py:253
  86.6 6.5 collective-permute-start.1
  93.1 6.5 collective-permute-start.2
  99.6 7.1 collective-permute-start.3
  106.7 6.6 collective-permute-start.4
  113.3 6.6 collective-permute-start.5
  120.0 6.8 collective-permute-start.6
  210.3 182.4 %copy-start.20 = (bf16[128,5,3,64]{0,3,2,1:T(8,128)(2,1)}, bf16[128,5,3,64]{0,3,2,1:T(8,128)(2,1)S(1)}, u32[]{:S(2)}) copy-start(bf16[128,5,3,64]{0,3,2,1:T(8,128)(2,1)S(1)} %fusion.78) | copy-start | bytes 737284
  210.4 7.7 copy-start.38
  210.4 7.7 copy-start.60
  211.1 8.3 copy-start.34
  211.1 8.3 copy-start.59
  211.4 9.4 copy-start.32
  211.4 9.4 copy-start.58
  329.5 51.6 %copy-start.26 = (bf16[128,960]{0,1:T(8,128)(2,1)S(1)}, bf16[128,960]{0,1:T(8,128)(2,1)}, u32[]{:S(2)}) copy-start(bf16[128,960]{0,1:T(8,128)(2,1)} %param.11) | copy-start | bytes 737284
  373.6 12.2 %slice-start = ((s8[4915200]{0:T(1024)(128)(4,1)}), s8[720896]{0:T(1024)(128)(4,1)S(1)}, s32[]{:S(2)}) async-start(s8[4915200]{0:T(1024)(128)(4,1)} %bitcast.539), calls=%async_computation.7 | async-start | bytes 1441792
  385.9 23.9 %copy-start.19 = (bf16[128,2560]{1,0:T(8,128)(2,1)}, bf16[128,2560]{1,0:T(8,128)(2,1)S(1)}, u32[]{:S(2)}) copy-start(bf16[128,2560]{1,0:T(8,128)(2,1)S(1)} %get-tuple-element.25) | copy-start | bytes 1966084
  391.7 64.6 %copy-start.5 = (f32[128,960]{0,1:T(8,128)}, f32[128,960]{0,1:T(8,128)S(1)}, u32[]{:S(2)}) copy-start(f32[128,960]{0,1:T(8,128)S(1)} %multiply_add_fusion) | copy-start | bytes 1474564
  409.8 7.7 collective-permute-start.7
  415.4 10.3 %copy-start.9 = (f32[5,3,128,128]{2,3,1,0:T(8,128)S(1)}, f32[5,3,128,128]{2,3,1,0:T(8,128)}, u32[]{:S(2)}) copy-start(f32[5,3,128,128]{2,3,1,0:T(8,128)} %fusion.60) | copy-start | bytes 2949124
  415.4 10.3 %copy-start.33 = (bf16[128,320]{0,1:T(8,128)(2,1)S(1)}, bf16[128,320]{0,1:T(8,128)(2,1)}, u32[]{:S(2)}) copy-start(bf16[128,320]{0,1:T(8,128)(2,1)} %get-tuple-element.34) | copy-start | bytes 245764
  417.5 7.7 collective-permute-start.8
  425.3 7.7 collective-permute-start.9
  425.6 22.9 %copy-start.52 = (f32[128,64]{0,1:T(8,128)S(1)}, f32[128,64]{0,1:T(8,128)}, u32[]{:S(2)}) copy-start(f32[128,64]{0,1:T(8,128)} %get-tuple-element.50) | copy-start | bytes 98308
  433.0 7.7 collective-permute-start.10
  433.4 23.0 %copy-start.21 = (bf16[128,5,3,64]{0,3,2,1:T(8,128)(2,1)S(1)}, bf16[128,5,3,64]{0,3,2,1:T(8,128)(2,1)}, u32[]{:S(2)}) copy-start(bf16[128,5,3,64]{0,3,2,1:T(8,128)(2,1)} %copy-done.20) | copy-start | bytes 737284
  440.8 7.7 collective-permute-start.11
  448.6 7.7 collective-permute-start.12
  448.6 15.5 %copy-start.54 = (f32[1,960]{1,0:T(1,128)S(1)}, f32[1,960]{1,0:T(1,128)}, u32[]{:S(2)}) copy-start(f32[1,960]{1,0:T(1,128)} %copy-done.53) | copy-start | bytes 11524
  448.6 15.5 %copy-start.57 = (f32[128]{0:T(128)S(1)}, f32[128]{0:T(128)}, u32[]{:S(2)}) copy-start(f32[128]{0:T(128)} %copy-done.56) | copy-start | bytes 1540
  448.7 18.1 %copy-start.22 = (bf16[128,960]{0,1:T(8,128)(2,1)}, bf16[128,960]{0,1:T(8,128)(2,1)S(1)}, u32[]{:S(2)}) copy-start(bf16[128,960]{0,1:T(8,128)(2,1)S(1)} %fusion.95) | copy-start | bytes 737284
  456.3 7.7 collective-permute-start.13
  464.1 7.7 collective-permute-start.14
  860.9 57.0 %collective-permute-start.15 = (f32[60,10240]{1,0:T(8,128)}, f32[60,10240]{1,0:T(8,128)}, u32[]{:S(2)}, u32[]{:S(2)}) collective-permute-start(f32[60,10240]{1,0:T(8,128)} %slice.178), channel_id=1, source_target_pairs={{0,8},{8,16},{16,24},{24,32},{32,40},{40,48},{48,56},{56,64},{64,7... | collective-permute-start | bytes 7372808
  933.4 57.7 %copy-start.6 = (f32[128,960]{0,1:T(8,128)S(1)}, f32[128,960]{0,1:T(8,128)}, u32[]{:S(2)}) copy-start(f32[128,960]{0,1:T(8,128)} %copy-done.5) | copy-start | bytes 1474564
  (44 other events, 164.1 us)
Sparse Core Ops, SparseCore 0:
  81.5 24.6 all-gather.14
  108.3 45.3 all-gather.18
  155.8 44.2 all-gather.16
  202.1 55.5 all-gather.20
  259.7 55.9 all-gather.22
  317.7 55.9 all-gather.24
  937.3 69.0 all-reduce.4
where the time goes:
time: 1030 us; the launch traced here: 1020 us
  blocking collectives  465 us (45%)
  waiting for transfers between devices  306 us (30%)
  local copies, waits for them, and re-layouts  106 us (10%)
  matrix products  76.8 us (7%)
  starting transfers between devices  40 us (4%)
  between operations  17.3 us (2%)
    unnamed x2, blocking collectives  384 us
    unnamed x151, local copies, waits for them, and re-layouts  51.5 us
    all_gather x1, waiting for transfers between devices, on_device(): lax.all_gather(shards[6], 'dp', axis=0, tiled=True)  50.6 us
    ppermute x8, waiting for transfers between devices, passed_along(): return lax.ppermute(block, axis, route)  46.5 us
    unnamed x8, waiting for transfers between devices  46.3 us
    all_gather x1, waiting for transfers between devices, on_device(): lax.all_gather(shards[7], 'dp', axis=0, tiled=True)  44.1 us
    all_gather x1, waiting for transfers between devices, on_device(): lax.all_gather(shards[1], 'dp', axis=0, tiled=True)  42.5 us
    concatenate x1, local copies, waits for them, and re-layouts, on_device(): stacked = jnp.concatenate(terms, axis=1)  41.3 us
  transfers between devices with their start and end apart: 23, of which 20 were waited for; matrix products, arithmetic and copies ran while one was open for 8% of the time, Pallas kernels for 0%

commit v1 on v0

--- a/solution.py
+++ b/solution.py
@@ -10,6 +10,14 @@
 EPS = 1e-05
 ROPE_BASE = 100000.0
 NEG_FILL = -1e30
+
+
+def gather_from_all(shard, axis, dim):
+    peers = lax.axis_size(axis)
+    repeats = [peers if d == dim else 1 for d in range(shard.ndim)]
+    return lax.all_to_all(
+        jnp.tile(shard, repeats), axis, split_axis=dim, concat_axis=dim, tiled=True
+    )
 
 
 def passed_along(block, axis, distance):
@@ -99,7 +107,7 @@
         lax.all_gather(shards[4], "dp", axis=0, tiled=True),
         lax.all_gather(shards[5], "dp", axis=0, tiled=True),
         lax.all_gather(shards[6], "dp", axis=0, tiled=True),
-        lax.all_gather(shards[7], "dp", axis=0, tiled=True),
+        gather_from_all(shards[7], "dp", 0),
     )
     gain_rows, query_mat, key_mat, value_mat, output_mat, gate_mat, up_mat, down_mat = gathered
     gain_first = gain_rows[0].astype(jnp.float32)

time: 1030 us -> 1060 us (1.029)
  waiting for transfers between devices: 306 us -> 330 us
  local copies, waits for them, and re-layouts: 106 us -> 117 us
    all_gather x1, waiting for transfers between devices: 24 us -> 55.2 us  [on_device(): lax.all_gather(shards[4], 'dp', axis=0, tiled=True)]
    unnamed x151 -> x153, local copies, waits for them, and re-layouts: 51.5 us -> 51.6 us
  transfers between devices with their start and end apart: 23 -> 24, of which waited for: 20 -> 20; matrix products, arithmetic and copies ran while one was open for 8% -> 48% of each run, Pallas kernels for 0% -> 0%
where the time goes in v1:
time: 1060 us
  blocking collectives  465 us (44%)
  waiting for transfers between devices  330 us (31%)
  local copies, waits for them, and re-layouts  117 us (11%)
  matrix products  76.7 us (7%)
  starting transfers between devices  42.6 us (4%)
  between operations  17.3 us (2%)
    unnamed x2, blocking collectives  384 us
    all_gather x1, waiting for transfers between devices, on_device(): lax.all_gather(shards[4], 'dp', axis=0, tiled=True)  55.2 us
    unnamed x153, local copies, waits for them, and re-layouts  51.6 us
    all_gather x1, waiting for transfers between devices, on_device(): lax.all_gather(shards[6], 'dp', axis=0, tiled=True)  50.6 us
    ppermute x8, waiting for transfers between devices, passed_along(): return lax.ppermute(block, axis, route)  46.5 us
    all_gather x1, waiting for transfers between devices, on_device(): lax.all_gather(shards[7], 'dp', axis=0, tiled=True)  44.1 us
    all_gather x1, waiting for transfers between devices, on_device(): lax.all_gather(shards[1], 'dp', axis=0, tiled=True)  42.5 us
    concatenate x1, local copies, waits for them, and re-layouts, on_device(): stacked = jnp.concatenate(terms, axis=1)  41.3 us
  transfers between devices with their start and end apart: 24, of which 20 were waited for; matrix products, arithmetic and copies ran while one was open for 48% of the time, Pallas kernels for 0%

profile of v1, /device:TPU:0, one launch (start us, length us, event | category | flops | bytes accessed | tf_op | source)
XLA Modules:
  0.0 1057.1 jit_solution(9065513755135200340)
XLA Ops:
  7.3 26.2 %all-gather.2 = bf16[16,60,320]{2,1,0:T(8,128)(2,1)S(1)} all-gather(bf16[1,60,320]{2,1,0:T(8,128)(2,1)} %bitcast.615), channel_id=1, replica_groups=mesh['dp'=16,'ctx'=8] {'dp'}, dimensions={0}, use_global_device_ids=true | all-gather | bytes 652800 | tf_op jit(solution)/shard_map/all_gather | solution.py:106
  33.7 19.7 %all-gather = bf16[16,60,2]{1,2,0:T(2,128)(2,1)S(1)} all-gather(bf16[1,60,2]{1,2,0:T(2,128)(2,1)} %bitcast.621), channel_id=1, replica_groups=mesh['dp'=16,'ctx'=8] {'dp'}, dimensions={0}, use_global_device_ids=true | all-gather | bytes 4080 | tf_op jit(solution)/shard_map/all_gather | solution.py:103
  55.2 22.4 %all-gather.1 = bf16[16,60,320]{2,1,0:T(8,128)(2,1)S(1)} all-gather(bf16[1,60,320]{2,1,0:T(8,128)(2,1)} %bitcast.616), channel_id=1, replica_groups=mesh['dp'=16,'ctx'=8] {'dp'}, dimensions={0}, use_global_device_ids=true | all-gather | bytes 652800 | tf_op jit(solution)/shard_map/all_gather | solution.py:105
  85.4 3.0 tile.2
  88.3 5.3 all-to-all-start
  95.5 3.9 collective-permute-start.1
  100.3 4.8 collective-permute-start.2
  106.1 5.6 collective-permute-start.3
  112.7 5.6 collective-permute-start.4
  119.4 5.6 collective-permute-start.5
  126.0 6.1 collective-permute-start.6
  135.7 55.2 %all-gather.19.cloned.1.call-done = bf16[16,60,960]{2,1,0:T(8,128)(2,1)} async-done(((bf16[1,60,960]{2,1,0:T(8,128)(2,1)}), bf16[16,60,960]{2,1,0:T(8,128)(2,1)}) %all-gather.19.cloned.1.call-update) | async-done | bytes 1843216 | tf_op jit(solution)/shard_map/all_gather | solution.py:107
  190.8 3.9 reshape.303
  194.8 42.5 %all-gather.17.cloned.1.call-done = bf16[16,60,960]{2,1,0:T(8,128)(2,1)} async-done(((bf16[1,60,960]{2,1,0:T(8,128)(2,1)}), bf16[16,60,960]{2,1,0:T(8,128)(2,1)}) %all-gather.17.cloned.1.call-update) | async-done | bytes 1843216 | tf_op jit(solution)/shard_map/all_gather | solution.py:104
  237.3 2.8 reshape.301
  259.3 35.5 %all-gather.21.cloned.1.call-done = bf16[16,60,2560]{2,1,0:T(8,128)(2,1)} async-done(((bf16[1,60,2560]{2,1,0:T(8,128)(2,1)}), bf16[16,60,2560]{2,1,0:T(8,128)(2,1)}) %all-gather.21.cloned.1.call-update) | async-done | bytes 4915216 | tf_op jit(solution)/shard_map/all_gather | solution.py:108
  294.9 7.3 reshape.305
  302.2 50.6 %all-gather.23.cloned.1.call-done = bf16[16,60,2560]{2,1,0:T(8,128)(2,1)} async-done(((bf16[1,60,2560]{2,1,0:T(8,128)(2,1)}), bf16[16,60,2560]{2,1,0:T(8,128)(2,1)}) %all-gather.23.cloned.1.call-update) | async-done | bytes 4915216 | tf_op jit(solution)/shard_map/all_gather | solution.py:109
  352.8 7.3 reshape.307
  360.1 4.5 fusion.147
  366.6 44.1 %all-gather.25.cloned.1.call-done = bf16[16,60,2560]{2,1,0:T(8,128)(2,1)} async-done(((bf16[1,60,2560]{2,1,0:T(8,128)(2,1)}), bf16[16,60,2560]{2,1,0:T(8,128)(2,1)}) %all-gather.25.cloned.1.call-update) | async-done | bytes 4915216 | tf_op jit(solution)/shard_map/all_gather | solution.py:179
  410.7 7.6 reshape.309
  418.3 4.7 multiply_convert_fusion
  424.5 4.1 multiply_reduce_fusion
  431.2 5.1 fusion.159
  436.3 5.2 fusion.160
  446.9 5.3 convolution_bitcast_fusion
  455.7 6.6 collective-permute-done.8
  463.1 7.0 collective-permute-done.9
  470.8 7.1 collective-permute-done.10
  478.3 7.3 collective-permute-done.11
  486.2 7.2 collective-permute-done.12
  496.0 5.1 collective-permute-done.13
  501.2 2.6 fusion.128
  503.9 5.1 collective-permute-done.14
  510.9 41.3 %concatenate.70 = f32[960,10240]{1,0:T(8,128)} concatenate(f32[960,960]{1,0:T(8,128)} %fusion.128, f32[960,320]{1,0:T(8,128)S(1)} %fusion.126, f32[960,320]{1,0:T(8,128)} %fusion.120, f32[960,960]{1,0:T(8,128)} %fusion.116, f32[960,2560]{1,0:T(8,128)} %fusion.159, f32[960,2560]{1,0:T(8,128)} %fusion.160, f32[960,2560]{1,0:T(8,128)} %convolution_bitcast_fusion), dimensions={1} | concatenate | bytes 78643200 | tf_op jit(solution)/shard_map/concatenate | solution.py:255
  552.2 344.0 %fusion = f32[64,10240]{1,0:T(8,128)S(1)} fusion(f32[960,10240]{1,0:T(8,128)} %concatenate.70), kind=kCustom, calls=%all-reduce-scatter | all-reduce-scatter fusion | flops 10485761 | bytes 41943552
  898.0 3.5 collective-permute-start.15
  903.4 7.3 all_to_all.7
  910.7 3.0 fusion.161
  913.7 4.7 fusion.74
  918.5 36.5 %collective-permute-done.15 = f32[60,10240]{1,0:T(8,128)} collective-permute-done((f32[60,10240]{1,0:T(8,128)}, f32[60,10240]{1,0:T(8,128)}, u32[]{:S(2)}, u32[]{:S(2)}) %collective-permute-start.15) | collective-permute-done | bytes 2457632
  954.9 15.6 %concatenate.71 = f32[124,10240]{1,0:T(8,128)} concatenate(f32[60,10240]{1,0:T(8,128)} %collective-permute-done.15, f32[64,10240]{1,0:T(8,128)S(1)} %fusion), dimensions={0} | concatenate | bytes 10158080
  970.5 3.8 constant_dynamic-slice_fusion
  975.2 40.0 %all-reduce = f32[2,960]{1,0:T(2,128)S(1)} all-reduce(f32[2,960]{1,0:T(2,128)S(1)} %pad_maximum_fusion.4), channel_id=2, replica_groups=mesh['dp'=16,'ctx'=8] {'dp'}, use_global_device_ids=true, to_apply=%region_9.10.clone | all-reduce | flops 1920 | bytes 15360
  1015.3 13.0 %psum.14 = f32[2,60]{1,0:T(2,128)} all-reduce(f32[2,60]{1,0:T(2,128)S(1)} %constant_dynamic-slice_fusion.1), channel_id=1, replica_groups=mesh['dp'=16,'ctx'=8] {'ctx'}, use_global_device_ids=true, to_apply=%region_10.11 | all-reduce | flops 120 | bytes 960 | tf_op jit(solution)/shard_map/psum | solution.py:261
  1029.2 14.4 %all-reduce.5.cloned.1.call-done = f32[60,10240]{1,0:T(8,128)} async-done(((f32[60,10240]{1,0:T(8,128)}), f32[60,10240]{1,0:T(8,128)}) %all-reduce.5.cloned.1.call-update) | async-done | bytes 2457616 | tf_op jit(solution)/shard_map/psum | solution.py:261
  1047.2 2.8 fusion.135
  (292 shorter events, 68.1 us)
Async XLA Ops:
  7.2 70.8 %copy-start.1 = (bf16[128,960]{0,1:T(8,128)(2,1)S(1)}, bf16[128,960]{0,1:T(8,128)(2,1)}, u32[]{:S(2)}) copy-start(bf16[128,960]{0,1:T(8,128)(2,1)} %param.10) | copy-start | bytes 737284
  7.2 126.3 %all-gather.15.cloned.1.call-start = ((), (), s32[]{:S(2)}) async-start(), calls=%async_computation.1 | async-start | bytes 1474560 | tf_op jit(solution)/shard_map/all_gather | solution.py:134
  33.4 51.9 %copy-start.26 = (bf16[60,2560]{1,0:T(8,128)(2,1)S(1)}, bf16[60,2560]{1,0:T(8,128)(2,1)}, u32[]{:S(2)}) copy-start(bf16[60,2560]{1,0:T(8,128)(2,1)} %param.19) | copy-start | bytes 921604
  33.7 54.6 %copy-start.17 = (bf16[960,320]{1,0:T(8,128)(2,1)}, bf16[960,320]{1,0:T(8,128)(2,1)S(1)}, u32[]{:S(2)}) copy-start(bf16[960,320]{1,0:T(8,128)(2,1)S(1)} %reshape.299) | copy-start | bytes 1843204
  54.1 25.9 %copy-start.54 = (f32[1,960]{1,0:T(1,128)}, f32[1,960]{1,0:T(1,128)S(1)}, u32[]{:S(2)}) copy-start(f32[1,960]{1,0:T(1,128)S(1)} %get-tuple-element.53) | copy-start | bytes 11524
  55.2 24.0 %copy-start.57 = (f32[128]{0:T(128)}, f32[128]{0:T(128)S(1)}, u32[]{:S(2)}) copy-start(f32[128]{0:T(128)S(1)} %add_rsqrt_fusion.1) | copy-start | bytes 1540
  77.9 10.4 copy-start.7
  78.6 9.8 copy-start.30
  81.4 109.4 %all-gather.19.cloned.1.call-start = ((), (), s32[]{:S(2)}) async-start(), calls=%async_computation.4 | async-start | bytes 2228224 | tf_op jit(solution)/shard_map/all_gather | solution.py:107
  82.2 155.2 %all-gather.17.cloned.1.call-start = ((), (), s32[]{:S(2)}) async-start(), calls=%async_computation.3 | async-start | bytes 2228224 | tf_op jit(solution)/shard_map/all_gather | solution.py:104
  82.9 212.0 %all-gather.21.cloned.1.call-start = ((), (), s32[]{:S(2)}) async-start(), calls=%async_computation.5 | async-start | bytes 5570560 | tf_op jit(solution)/shard_map/all_gather | solution.py:108
  83.5 269.3 %all-gather.23.cloned.1.call-start = ((), (), s32[]{:S(2)}) async-start(), calls=%async_computation.6 | async-start | bytes 5570560 | tf_op jit(solution)/shard_map/all_gather | solution.py:109
  84.0 11.4 %collective-permute-start = (bf16[128,640]{0,1:T(8,128)(2,1)}, bf16[128,640]{0,1:T(8,128)(2,1)S(1)}, u32[]{:S(2)}, u32[]{:S(2)}) collective-permute-start(bf16[128,640]{0,1:T(8,128)(2,1)} %pad_maximum_fusion.1), channel_id=1, source_target_pairs={{0,1},{1,2},{2,3},{3,4},{4,5},{5,6},{6,7},{8,9},{9,10},{10,11},{11... | collective-permute-start | bytes 491528 | tf_op jit(solution)/shard_map/ppermute | solution.py:32
  88.3 815.0 %all-to-all-start = ((bf16[16,60,2560]{2,1,0:T(8,128)(2,1)}), bf16[16,60,2560]{2,1,0:T(8,128)(2,1)}, u32[]{:S(2)}, u32[]{:S(2)}) async-start(bf16[16,60,2560]{2,1,0:T(8,128)(2,1)} %tile.2), calls=%async_computation | async-start | bytes 10485760 | tf_op jit(solution)/shard_map/all_to_all | solution.py:18
  93.7 317.0 %all-gather.25.cloned.1.call-start = ((), (), s32[]{:S(2)}) async-start(), calls=%async_computation.7 | async-start | bytes 5570560 | tf_op jit(solution)/shard_map/all_gather | solution.py:179
  94.3 949.3 %all-reduce.5.cloned.1.call-start = ((), (), s32[]{:S(2)}) async-start(), calls=%async_computation.2 | async-start | bytes 5242880 | tf_op jit(solution)/shard_map/psum | solution.py:261
  95.5 4.9 collective-permute-start.1
  100.3 5.8 collective-permute-start.2
  106.1 6.6 collective-permute-start.3
  112.7 6.6 collective-permute-start.4
  119.4 6.6 collective-permute-start.5
  126.0 6.8 collective-permute-start.6
  247.4 182.4 %copy-start.20 = (bf16[128,5,3,64]{0,3,2,1:T(8,128)(2,1)}, bf16[128,5,3,64]{0,3,2,1:T(8,128)(2,1)S(1)}, u32[]{:S(2)}) copy-start(bf16[128,5,3,64]{0,3,2,1:T(8,128)(2,1)S(1)} %fusion.78) | copy-start | bytes 737284
  248.3 8.4 copy-start.35
  248.3 8.4 copy-start.60
  248.5 9.4 copy-start.33
  248.5 9.4 copy-start.59
  366.6 51.7 %copy-start.27 = (bf16[128,960]{0,1:T(8,128)(2,1)S(1)}, bf16[128,960]{0,1:T(8,128)(2,1)}, u32[]{:S(2)}) copy-start(bf16[128,960]{0,1:T(8,128)(2,1)} %param.11) | copy-start | bytes 737284
  410.7 12.3 %slice-start = ((s8[4915200]{0:T(1024)(128)(4,1)}), s8[720896]{0:T(1024)(128)(4,1)S(1)}, s32[]{:S(2)}) async-start(s8[4915200]{0:T(1024)(128)(4,1)} %bitcast.539), calls=%async_computation.8 | async-start | bytes 1441792
  423.0 23.9 %copy-start.19 = (bf16[128,2560]{1,0:T(8,128)(2,1)}, bf16[128,2560]{1,0:T(8,128)(2,1)S(1)}, u32[]{:S(2)}) copy-start(bf16[128,2560]{1,0:T(8,128)(2,1)S(1)} %get-tuple-element.25) | copy-start | bytes 1966084
  428.8 64.6 %copy-start.5 = (f32[128,960]{0,1:T(8,128)}, f32[128,960]{0,1:T(8,128)S(1)}, u32[]{:S(2)}) copy-start(f32[128,960]{0,1:T(8,128)S(1)} %multiply_add_fusion) | copy-start | bytes 1474564
  446.9 7.7 collective-permute-start.7
  452.5 10.2 copy-start.9
  452.5 10.2 copy-start.34
  454.6 7.7 collective-permute-start.8
  462.4 7.7 collective-permute-start.9
  462.7 22.9 %copy-start.53 = (f32[128,64]{0,1:T(8,128)S(1)}, f32[128,64]{0,1:T(8,128)}, u32[]{:S(2)}) copy-start(f32[128,64]{0,1:T(8,128)} %get-tuple-element.50) | copy-start | bytes 98308
  470.1 7.7 collective-permute-start.10
  470.5 23.0 %copy-start.21 = (bf16[128,5,3,64]{0,3,2,1:T(8,128)(2,1)S(1)}, bf16[128,5,3,64]{0,3,2,1:T(8,128)(2,1)}, u32[]{:S(2)}) copy-start(bf16[128,5,3,64]{0,3,2,1:T(8,128)(2,1)} %copy-done.20) | copy-start | bytes 737284
  477.9 7.7 collective-permute-start.11
  485.7 7.7 collective-permute-start.12
  485.7 15.5 %copy-start.55 = (f32[1,960]{1,0:T(1,128)S(1)}, f32[1,960]{1,0:T(1,128)}, u32[]{:S(2)}) copy-start(f32[1,960]{1,0:T(1,128)} %copy-done.54) | copy-start | bytes 11524
  485.7 15.5 %copy-start.58 = (f32[128]{0:T(128)S(1)}, f32[128]{0:T(128)}, u32[]{:S(2)}) copy-start(f32[128]{0:T(128)} %copy-done.57) | copy-start | bytes 1540
  485.8 18.0 %copy-start.22 = (bf16[128,960]{0,1:T(8,128)(2,1)}, bf16[128,960]{0,1:T(8,128)(2,1)S(1)}, u32[]{:S(2)}) copy-start(bf16[128,960]{0,1:T(8,128)(2,1)S(1)} %fusion.95) | copy-start | bytes 737284
  493.4 7.7 collective-permute-start.13
  501.2 7.7 collective-permute-start.14
  898.0 57.0 %collective-permute-start.15 = (f32[60,10240]{1,0:T(8,128)}, f32[60,10240]{1,0:T(8,128)}, u32[]{:S(2)}, u32[]{:S(2)}) collective-permute-start(f32[60,10240]{1,0:T(8,128)} %slice.178), channel_id=1, source_target_pairs={{0,8},{8,16},{16,24},{24,32},{32,40},{40,48},{48,56},{56,64},{64,7... | collective-permute-start | bytes 7372808
  970.5 57.7 %copy-start.6 = (f32[128,960]{0,1:T(8,128)S(1)}, f32[128,960]{0,1:T(8,128)}, u32[]{:S(2)}) copy-start(f32[128,960]{0,1:T(8,128)} %copy-done.5) | copy-start | bytes 1474564
  (46 other events, 180.0 us)
Sparse Core Ops, SparseCore 0:
  81.5 23.5 all-gather.14
  107.3 83.5 all-gather.18
  193.0 44.2 all-gather.16
  239.3 55.5 all-gather.20
  296.8 55.9 all-gather.22
  354.8 55.9 all-gather.24
  974.4 69.0 all-reduce.4
